TPU v7x, 32 devices: a whole 2x2x4 slice. The times are simulated.
32 devices in a mesh: ctx: 8 (over y, x, core), fsdp: 4 (over z).
Axes of the slice: x: 2, y: 2, z: 4, core: 2. Of those that a mesh axis runs over, the one named last changes fastest.
Arguments:
- layer_in: bfloat16 [8, 1024, 1024], P('fsdp', 'ctx'), may hold values from -6 to 6
- cotangent: bfloat16 [8, 1024, 1024], P('fsdp', 'ctx'), may hold values from -6 to 6
- norm1_gain: bfloat16 [1024], P('fsdp'), may hold values from 0.099609375 to 1.8984375
- norm1_shift: bfloat16 [1024], P('fsdp'), may hold values from -3 to 3
- norm2_gain: bfloat16 [1024], P('fsdp'), may hold values from 0.099609375 to 1.8984375
- norm2_shift: bfloat16 [1024], P('fsdp'), may hold values from -3 to 3
- qkv_weight: bfloat16 [1024, 3072], P('fsdp'), may hold values from -4 to 4
- qv_bias: bfloat16 [2048], P('fsdp'), may hold values from -3 to 3
- key_bias: bfloat16 [256], P('fsdp'), may hold values from -3 to 3
- attn_out_weight: bfloat16 [1024, 1024], P('fsdp'), may hold values from -1.5 to 1.5
- attn_out_bias: bfloat16 [1024], P('fsdp'), may hold values from -3 to 3
- ff_in_weight: bfloat16 [1024, 4096], P('fsdp'), may hold values from -0.1875 to 0.1875
- ff_in_bias: bfloat16 [4096], P('fsdp'), may hold values from -3 to 3
- ff_out_weight: bfloat16 [1024, 4096], P('fsdp'), may hold values from -0.09375 to 0.09375
- ff_out_bias: bfloat16 [1024], P('fsdp'), may hold values from -3 to 3
Outputs:
- layer_out: bfloat16 [8, 1024, 1024], P('fsdp', 'ctx')
- input_grad: float32 [8, 1024, 1024], P('fsdp', 'ctx')
- norm1_gain_grad: float32 [1024], P('fsdp')
- norm1_shift_grad: float32 [1024], P('fsdp')
- norm2_gain_grad: float32 [1024], P('fsdp')
- norm2_shift_grad: float32 [1024], P('fsdp')
- qkv_weight_grad: float32 [1024, 3072], P('fsdp')
- qv_bias_grad: float32 [2048], P('fsdp')
- key_bias_grad: float32 [256], P('fsdp')
- attn_out_weight_grad: float32 [1024, 1024], P('fsdp')
- attn_out_bias_grad: float32 [1024], P('fsdp')
- ff_in_weight_grad: float32 [1024, 4096], P('fsdp')
- ff_in_bias_grad: float32 [4096], P('fsdp')
- ff_out_weight_grad: float32 [1024, 4096], P('fsdp')
- ff_out_bias_grad: float32 [1024], P('fsdp')
All inputs are finite; a program needn't handle non-finite values.
Results may differ from a plain program's by a relative error of at most 0.025.
Values may be sent and summed in bfloat16 or wider, within the bound.
A program may use at most 256 MiB of HBM per device.

v0:
```python
import math

import jax
import jax.numpy as jnp
from jax import lax
from jax.sharding import PartitionSpec as P

D = 1024
H = 16
HD = 64
ROT = 16


EPSILON = 1e-05


def layer_norm(inputs, gain_vec, shift_vec):
    average = jnp.mean(inputs, axis=-1, keepdims=True)
    centred = inputs - average
    variance = jnp.mean(centred * centred, axis=-1, keepdims=True)
    inverse = lax.rsqrt(variance + EPSILON)
    normed = centred * inverse
    return (normed * gain_vec + shift_vec, normed, inverse)


def norm_back(upstream, normed, inverse, gain_vec):
    gain_grad = jnp.sum(upstream * normed, axis=0)
    shift_grad = jnp.sum(upstream, axis=0)
    scaled = upstream * gain_vec
    inner = (
        scaled
        - jnp.mean(scaled, axis=-1, keepdims=True)
        - normed * jnp.mean(scaled * normed, axis=-1, keepdims=True)
    )
    return (inverse * inner, gain_grad, shift_grad)


def paired_position(row_ids, half_rows, groups):
    owner = row_ids // (2 * half_rows)
    within = row_ids % (2 * half_rows)
    late = 2 * half_rows * groups - (owner + 2) * half_rows + within
    return jnp.where(within < half_rows, owner * half_rows + within, late)


def rotary_tables(positions):
    halfway = ROT // 2
    freq_steps = jnp.arange(halfway, dtype=jnp.float32)
    frequency = jnp.exp(freq_steps * (-2.0 * math.log(10000.0) / ROT))
    theta = positions.astype(jnp.float32)[:, None] * frequency[None, :]
    return (jnp.cos(theta)[:, None, :], jnp.sin(theta)[:, None, :])


def rotate(inputs, cosine, sine):
    halfway = ROT // 2
    first = inputs[..., :halfway]
    second = inputs[..., halfway:ROT]
    return jnp.concatenate(
        [first * cosine - second * sine, second * cosine + first * sine, inputs[..., ROT:]], axis=-1
    )


def rotate_back(upstream, cosine, sine):
    halfway = ROT // 2
    first = upstream[..., :halfway]
    second = upstream[..., halfway:ROT]
    return jnp.concatenate(
        [first * cosine + second * sine, second * cosine - first * sine, upstream[..., ROT:]],
        axis=-1,
    )


def gelu_parts(inputs):
    cumulative = 0.5 * (1.0 + lax.erf(inputs * (1.0 / math.sqrt(2.0))))
    density = jnp.exp(-0.5 * inputs * inputs) * (1.0 / math.sqrt(2.0 * math.pi))
    return (inputs * cumulative, cumulative + inputs * density)


def contract_rows(left, right):
    return lax.dot_general(
        left, right, (((0,), (0,)), ((), ())), preferred_element_type=jnp.float32
    )


def contract_cols(left, right):
    return lax.dot_general(
        left, right, (((1,), (1,)), ((), ())), preferred_element_type=jnp.float32
    )


def blocked(matrix, blocks, key_block):
    seq_count = matrix.shape[0]
    return matrix.reshape(seq_count, blocks, key_block, H, HD).transpose(1, 0, 2, 3, 4)


def per_device(
    layer_in,
    cotangent,
    norm1_gain,
    norm1_shift,
    norm2_gain,
    norm2_shift,
    qkv_weight,
    qv_bias,
    key_bias,
    attn_out_weight,
    attn_out_bias,
    ff_in_weight,
    ff_in_bias,
    ff_out_weight,
    ff_out_bias,
):
    ctx_count = lax.axis_size("ctx")
    shard_count = lax.axis_size("fsdp")
    ctx_place = lax.axis_index("ctx")
    shard_place = lax.axis_index("fsdp")
    seq_count = layer_in.shape[0]
    tokens = layer_in.shape[1]
    half_rows = tokens // 2
    row_total = seq_count * tokens
    inputs_f = layer_in.reshape(row_total, D).astype(jnp.float32)
    upstream = cotangent.reshape(row_total, D)
    upstream_f = upstream.astype(jnp.float32)
    gathered = (
        lax.all_gather(norm1_gain, "fsdp", axis=0, tiled=True),
        lax.all_gather(norm1_shift, "fsdp", axis=0, tiled=True),
        lax.all_gather(norm2_gain, "fsdp", axis=0, tiled=True),
        lax.all_gather(norm2_shift, "fsdp", axis=0, tiled=True),
        lax.all_gather(qv_bias, "fsdp", axis=0, tiled=True),
        lax.all_gather(key_bias, "fsdp", axis=0, tiled=True),
        lax.all_gather(attn_out_bias, "fsdp", axis=0, tiled=True),
        lax.all_gather(ff_in_bias, "fsdp", axis=0, tiled=True),
        lax.all_gather(ff_out_bias, "fsdp", axis=0, tiled=True),
    )
    (
        gain_one,
        shift_one,
        gain_two,
        shift_two,
        query_value_bias,
        rotary_bias,
        attn_bias,
        ff_bias,
        out_bias,
    ) = [piece.astype(jnp.float32) for piece in gathered]
    key_full = jnp.concatenate(
        [rotary_bias.reshape(H, ROT), jnp.zeros((H, HD - ROT), jnp.float32)], axis=1
    ).reshape(D)
    in_bias = jnp.concatenate([query_value_bias[:D], key_full, query_value_bias[D:]])
    qkv_full, ff_in_full, attn_out_full, ff_out_full = (
        lax.all_gather(qkv_weight, "fsdp", axis=0, tiled=True),
        lax.all_gather(ff_in_weight, "fsdp", axis=0, tiled=True),
        lax.all_gather(attn_out_weight, "fsdp", axis=0, tiled=True),
        lax.all_gather(ff_out_weight, "fsdp", axis=0, tiled=True),
    )
    query_pos = paired_position(
        jnp.arange(tokens, dtype=jnp.int32) + ctx_place * tokens, half_rows, ctx_count
    )
    cosine, sine = rotary_tables(query_pos)
    normed_one, unit_one, inverse_one = layer_norm(inputs_f, gain_one, shift_one)
    normed_two, unit_two, inverse_two = layer_norm(inputs_f, gain_two, shift_two)
    one_b = normed_one.astype(jnp.bfloat16)
    two_b = normed_two.astype(jnp.bfloat16)
    projected = jnp.dot(one_b, qkv_full, preferred_element_type=jnp.float32) + in_bias
    ff_pre = jnp.dot(two_b, ff_in_full, preferred_element_type=jnp.float32) + ff_bias
    query_b = rotate(projected[:, :D].reshape(seq_count, tokens, H, HD), cosine, sine).astype(
        jnp.bfloat16
    )
    keys_b = rotate(projected[:, D : 2 * D].reshape(seq_count, tokens, H, HD), cosine, sine).astype(
        jnp.bfloat16
    )
    values_b = projected[:, 2 * D :].astype(jnp.bfloat16).reshape(seq_count, tokens, D)
    all_keys, all_values = (
        lax.all_gather(keys_b.reshape(seq_count, tokens, D), "ctx", axis=1, tiled=True),
        lax.all_gather(values_b, "ctx", axis=1, tiled=True),
    )
    key_total = all_keys.shape[1]
    key_block = math.gcd(key_total, 512)
    blocks = key_total // key_block
    key_pos = paired_position(jnp.arange(key_total, dtype=jnp.int32), half_rows, ctx_count).reshape(
        blocks, key_block
    )
    keys_blocked = blocked(all_keys, blocks, key_block)
    values_blocked = blocked(all_values, blocks, key_block)

    def block_scores(key_piece, pos_piece):
        scores = (
            jnp.einsum("sqhd,skhd->shqk", query_b, key_piece, preferred_element_type=jnp.float32)
            * 0.125
        )
        allowed = pos_piece[None, None, None, :] <= query_pos[None, None, :, None]
        return (jnp.where(allowed, scores, -1e30), allowed)

    def first_pass(state, inputs):
        highest, total = state
        scores, allowed = block_scores(inputs[0], inputs[1])
        new_high = jnp.maximum(highest, jnp.max(scores, axis=-1))
        total = total * jnp.exp(highest - new_high) + jnp.sum(
            jnp.exp(scores - new_high[..., None]), axis=-1
        )
        return ((new_high, total), None)

    start_state = (
        jnp.full((seq_count, H, tokens), -1e30, jnp.float32),
        jnp.zeros((seq_count, H, tokens), jnp.float32),
    )
    (highest, total), unused = lax.scan(first_pass, start_state, (keys_blocked, key_pos))
    log_total = highest + jnp.log(total)

    def second_pass(mixed, inputs):
        scores, allowed = block_scores(inputs[0], inputs[2])
        weights = jnp.where(allowed, jnp.exp(scores - log_total[..., None]), 0.0).astype(
            jnp.bfloat16
        )
        return (
            mixed
            + jnp.einsum("shqk,skhd->sqhd", weights, inputs[1], preferred_element_type=jnp.float32),
            None,
        )

    mixed, unused = lax.scan(
        second_pass,
        jnp.zeros((seq_count, tokens, H, HD), jnp.float32),
        (keys_blocked, values_blocked, key_pos),
    )
    attn_b = mixed.reshape(row_total, D).astype(jnp.bfloat16)
    activation, slope = gelu_parts(ff_pre)
    gelu_b = activation.astype(jnp.bfloat16)
    act_cat = jnp.concatenate([attn_b, gelu_b], axis=1)
    out_cat = jnp.concatenate([attn_out_full, ff_out_full], axis=1)
    mixture = contract_cols(act_cat, out_cat)
    layer_out = (inputs_f + mixture + attn_bias + out_bias).astype(jnp.bfloat16)
    back_cat = jnp.dot(upstream, out_cat, preferred_element_type=jnp.float32)
    dout_b = back_cat[:, :D].astype(jnp.bfloat16).reshape(seq_count, tokens, H, HD)
    dpre = back_cat[:, D:] * slope
    dpre_b = dpre.astype(jnp.bfloat16)
    delta = jnp.sum(
        dout_b.astype(jnp.float32) * attn_b.astype(jnp.float32).reshape(seq_count, tokens, H, HD),
        axis=-1,
    ).transpose(0, 2, 1)

    def query_side(dquery, inputs):
        key_piece, value_piece, pos_piece = inputs
        scores, allowed = block_scores(key_piece, pos_piece)
        probs = jnp.where(allowed, jnp.exp(scores - log_total[..., None]), 0.0)
        dprobs = jnp.einsum(
            "sqhd,skhd->shqk", dout_b, value_piece, preferred_element_type=jnp.float32
        )
        dscores = (probs * (dprobs - delta[..., None])).astype(jnp.bfloat16)
        dquery = (
            dquery
            + jnp.einsum("shqk,skhd->sqhd", dscores, key_piece, preferred_element_type=jnp.float32)
            * 0.125
        )
        return (dquery, (probs, dscores))

    zero_query = jnp.zeros((seq_count, tokens, H, HD), jnp.float32)

    def dquery_pass(dquery, inputs):
        dquery, unused_pair = query_side(dquery, inputs)
        return (dquery, None)

    dquery, unused = lax.scan(dquery_pass, zero_query, (keys_blocked, values_blocked, key_pos))
    all_query, all_dout = (
        lax.all_gather(query_b.reshape(seq_count, tokens, D), "ctx", axis=1, tiled=True),
        lax.all_gather(dout_b.reshape(seq_count, tokens, D), "ctx", axis=1, tiled=True),
    )
    all_lse, all_delta = (
        lax.all_gather(log_total, "ctx", axis=2, tiled=True),
        lax.all_gather(delta, "ctx", axis=2, tiled=True),
    )
    own_values = values_b.reshape(seq_count, tokens, H, HD)
    query_blocked = blocked(all_query, blocks, key_block)
    dout_blocked = blocked(all_dout, blocks, key_block)
    lse_blocked = all_lse.reshape(seq_count, H, blocks, key_block).transpose(2, 0, 1, 3)
    delta_blocked = all_delta.reshape(seq_count, H, blocks, key_block).transpose(2, 0, 1, 3)

    def key_pass(sums, inputs):
        key_sum, value_sum = sums
        rows_q, rows_do, rows_lse, rows_delta, pos_q = inputs
        scores = (
            jnp.einsum("sqhd,skhd->shqk", rows_q, keys_b, preferred_element_type=jnp.float32)
            * 0.125
        )
        allowed = query_pos[None, None, None, :] <= pos_q[None, None, :, None]
        probs = jnp.where(
            allowed, jnp.exp(jnp.where(allowed, scores, -1e30) - rows_lse[..., None]), 0.0
        )
        dprobs = jnp.einsum(
            "sqhd,skhd->shqk", rows_do, own_values, preferred_element_type=jnp.float32
        )
        dscores = (probs * (dprobs - rows_delta[..., None])).astype(jnp.bfloat16)
        key_sum = (
            key_sum
            + jnp.einsum("shqk,sqhd->skhd", dscores, rows_q, preferred_element_type=jnp.float32)
            * 0.125
        )
        value_sum = value_sum + jnp.einsum(
            "shqk,sqhd->skhd",
            probs.astype(jnp.bfloat16),
            rows_do,
            preferred_element_type=jnp.float32,
        )
        return ((key_sum, value_sum), None)

    (dkey_own, dvalue_own), unused = lax.scan(
        key_pass,
        (zero_query, zero_query),
        (query_blocked, dout_blocked, lse_blocked, delta_blocked, key_pos),
    )
    dquery_pre = rotate_back(dquery, cosine, sine).reshape(row_total, D)
    dkey_pre = rotate_back(dkey_own, cosine, sine)
    dvalue_rows = dvalue_own.reshape(row_total, D)
    dproj = jnp.concatenate([dquery_pre, dkey_pre.reshape(row_total, D), dvalue_rows], axis=1)
    dproj_b = dproj.astype(jnp.bfloat16)
    dnormed_one = contract_cols(dproj_b, qkv_full)
    dnormed_two = contract_cols(dpre_b, ff_in_full)
    dinput_one, gain_grad_one, shift_grad_one = norm_back(
        dnormed_one, unit_one, inverse_one, gain_one
    )
    dinput_two, gain_grad_two, shift_grad_two = norm_back(
        dnormed_two, unit_two, inverse_two, gain_two
    )
    input_grad = (upstream_f + dinput_one + dinput_two).reshape(seq_count, tokens, D)

    def make_terms(cot_left, one_left, two_left):

        def out_term(start, count):
            return contract_rows(cot_left, act_cat)

        def in_term(start, count):
            return jnp.concatenate(
                [contract_rows(one_left, dproj_b), contract_rows(two_left, dpre_b)], axis=1
            )

        return (out_term, in_term)

    row_count = D // shard_count
    out_term, in_term = make_terms(upstream, one_b, two_b)
    out_part = lax.psum_scatter(
        out_term(jnp.int32(0), row_count * lax.axis_size("fsdp")).astype(jnp.bfloat16),
        "fsdp",
        scatter_dimension=0,
        tiled=True,
    ).astype(jnp.float32)
    in_part = lax.psum_scatter(
        in_term(jnp.int32(0), row_count * lax.axis_size("fsdp")).astype(jnp.bfloat16),
        "fsdp",
        scatter_dimension=0,
        tiled=True,
    ).astype(jnp.float32)
    out_part, in_part = (
        lax.psum(out_part.astype(jnp.bfloat16), "ctx").astype(jnp.float32),
        lax.psum(in_part.astype(jnp.bfloat16), "ctx").astype(jnp.float32),
    )
    qv_grad = jnp.concatenate([jnp.sum(dquery_pre, axis=0), jnp.sum(dvalue_rows, axis=0)])
    rotary_grad = jnp.sum(dkey_pre[..., :ROT], axis=(0, 1)).reshape(H * ROT)
    cot_grad = jnp.sum(upstream_f, axis=0)
    ff_bias_grad = jnp.sum(dpre, axis=0)
    summed = lax.psum(
        (
            gain_grad_one,
            shift_grad_one,
            gain_grad_two,
            shift_grad_two,
            qv_grad,
            rotary_grad,
            cot_grad,
            ff_bias_grad,
        ),
        ("ctx", "fsdp"),
    )

    def own_share(vector):
        width = vector.shape[0] // shard_count
        return lax.dynamic_slice_in_dim(vector, shard_place * width, width, 0)

    shares = [own_share(vector) for vector in summed]
    return (
        layer_out.reshape(seq_count, tokens, D),
        input_grad,
        shares[0],
        shares[1],
        shares[2],
        shares[3],
        in_part[:, : 3 * D],
        shares[4],
        shares[5],
        out_part[:, :D],
        shares[6],
        in_part[:, 3 * D :],
        shares[7],
        out_part[:, D:],
        shares[6],
    )


def solution(mesh):
    placed = (
        P("fsdp", "ctx", None),
        P("fsdp", "ctx", None),
        P("fsdp"),
        P("fsdp"),
        P("fsdp"),
        P("fsdp"),
        P("fsdp", None),
        P("fsdp"),
        P("fsdp"),
        P("fsdp", None),
        P("fsdp"),
        P("fsdp", None),
        P("fsdp"),
        P("fsdp", None),
        P("fsdp"),
    )
    return jax.shard_map(
        per_device,
        mesh=mesh,
        in_specs=placed,
        out_specs=(
            P("fsdp", "ctx", None),
            P("fsdp", "ctx", None),
            P("fsdp"),
            P("fsdp"),
            P("fsdp"),
            P("fsdp"),
            P("fsdp", None),
            P("fsdp"),
            P("fsdp"),
            P("fsdp", None),
            P("fsdp"),
            P("fsdp", None),
            P("fsdp"),
            P("fsdp", None),
            P("fsdp"),
        ),
        check_vma=False,
    )
```

profile of v0, /device:TPU:0, one launch (start us, length us, event | category | flops | bytes accessed | tf_op | source)
XLA Modules:
  0.0 1189.8 jit_solution(6554706821487634734)
XLA Ops:
  10.1 12.7 %all-gather.1 = bf16[4,1,256]{2,1,0:T(2,128)(2,1)S(1)} all-gather(bf16[1,1,256]{2,1,0:T(2,128)(2,1)S(1)} %reshape.446), channel_id=1, replica_groups=mesh['ctx'=8,'fsdp'=4] {'fsdp'}, dimensions={0}, use_global_device_ids=true | all-gather | bytes 2560 | tf_op jit(solution)/shard_map/all_gather | solution.py:125
  22.8 8.1 all-gather
  30.9 14.0 %all-gather.4 = bf16[4,1,256]{2,1,0:T(2,128)(2,1)S(1)} all-gather(bf16[1,1,256]{2,1,0:T(2,128)(2,1)S(1)} %reshape.452), channel_id=1, replica_groups=mesh['ctx'=8,'fsdp'=4] {'fsdp'}, dimensions={0}, use_global_device_ids=true | all-gather | bytes 2560 | tf_op jit(solution)/shard_map/all_gather | solution.py:127
  45.0 8.7 all-gather.3
  55.2 10.4 all-reduce.1
  65.7 22.4 %all-gather.2 = bf16[4,1,512]{2,1,0:T(2,128)(2,1)S(1)} all-gather(bf16[1,1,512]{2,1,0:T(2,128)(2,1)S(1)} %reshape.448), channel_id=1, replica_groups=mesh['ctx'=8,'fsdp'=4] {'fsdp'}, dimensions={0}, use_global_device_ids=true | all-gather | bytes 5120 | tf_op jit(solution)/shard_map/all_gather | solution.py:128
  90.4 37.9 %all-gather.16.cloned.1.call-done = bf16[1024,3072]{1,0:T(8,128)(2,1)} async-done(((bf16[256,3072]{1,0:T(8,128)(2,1)}), bf16[1024,3072]{1,0:T(8,128)(2,1)}) %all-gather.16.cloned.1.call-update) | async-done | bytes 6291472 | tf_op jit(solution)/shard_map/all_gather | solution.py:150
  150.8 12.4 %all_gather.67 = bf16[4096]{0:T(1024)(128)(2,1)S(1)} all-gather(bf16[1024]{0:T(1024)(128)(2,1)S(1)} %copy-done.39), channel_id=1, replica_groups=mesh['ctx'=8,'fsdp'=4] {'fsdp'}, dimensions={0}, use_global_device_ids=true | all-gather | bytes 10240 | tf_op jit(solution)/shard_map/all_gather | solution.py:131
  163.2 10.6 all-gather.24.cloned.1.call-done
  177.0 146.9 %all-gather.26.cloned.1.call-done = bf16[1024,4096]{1,0:T(8,128)(2,1)} async-done(((bf16[256,4096]{1,0:T(8,128)(2,1)}), bf16[1024,4096]{1,0:T(8,128)(2,1)}) %all-gather.26.cloned.1.call-update) | async-done | bytes 8388624 | tf_op jit(solution)/shard_map/all_gather | solution.py:153
  323.8 8.3 constant_dynamic-update-slice_fusion
  342.8 130.3 %all-gather.22.cloned.1.call-done = bf16[1024,4096]{1,0:T(8,128)(2,1)} async-done(((bf16[256,4096]{1,0:T(8,128)(2,1)}), bf16[1024,4096]{1,0:T(8,128)(2,1)}) %all-gather.22.cloned.1.call-update) | async-done | bytes 8388624 | tf_op jit(solution)/shard_map/all_gather | solution.py:151
  473.1 9.2 fusion.167
  482.3 28.6 %all-gather.18.cloned.1.call-done = bf16[2,1024,1024]{1,2,0:T(8,128)(2,1)} async-done(((bf16[2,128,1024]{1,2,0:T(8,128)(2,1)}), bf16[2,1024,1024]{1,2,0:T(8,128)(2,1)}) %all-gather.18.cloned.1.call-update) | async-done | bytes 4194320 | tf_op jit(solution)/shard_map/all_gather | solution.py:174
  524.2 25.9 %all-gather.20.cloned.1.call-done = bf16[2,1024,1024]{1,2,0:T(8,128)(2,1)} async-done(((bf16[2,128,1024]{1,2,0:T(8,128)(2,1)}), bf16[2,1024,1024]{1,2,0:T(8,128)(2,1)}) %all-gather.20.cloned.1.call-update) | async-done | bytes 4194320 | tf_op jit(solution)/shard_map/all_gather | solution.py:173
  563.5 24.2 %while.48 = (s32[]{:T(128)}, f32[2,16,128]{2,1,0:T(8,128)S(1)}, f32[2,16,128]{2,1,0:T(8,128)S(1)}, s32[2,512]{1,0:T(2,128)S(1)}, bf16[2,2,512,16,64]{2,4,3,1,0:T...) while((s32[]{:T(128)}, f32[2,16,128]{2,1,0:T(8,128)S(1)}, ...), condition=%wide.region_5.6_spmd.clone, body=%wide.region_2.5_spmd.clone.sunk | while | flops 283205120 | bytes 19815548 | solution.py:206
  587.7 13.5 %while.49 = (s32[]{:T(128)}, f32[2,128,16,64]{1,3,2,0:T(8,128)}, bf16[2,2,512,16,64]{2,4,3,1,0:T(8,128)(2,1)}, s32[2,512]{1,0:T(2,128)S(1)}, bf16[2,2,512,16,64]...) while((s32[]{:T(128)}, f32[2,128,16,64]{1,3,2,0:T(8,128)}, ...), condition=%wide.region_7.8_spmd.clone, body=%wide.region_6.7_spmd.clone.sunk | while | flops 547950080 | bytes 6972030 | solution.py:220
  625.0 30.8 %while.50 = (s32[]{:T(128)}, f32[2,128,16,64]{1,3,2,0:T(8,128)S(1)}, bf16[2,2,512,16,64]{2,4,3,1,0:T(8,128)(2,1)}, s32[2,512]{1,0:T(2,128)S(1)}, bf16[2,128,16,6...) while((s32[]{:T(128)}, ...), condition=%wide.region_10.11_spmd.clone, body=%wide.region_9.10_spmd.clone.sunk | while | flops 820841984 | bytes 26387088 | solution.py:262
  631.6 8.8 fusion.237
  646.9 8.9 fusion.237
  670.7 9.3 all_gather.73
  680.1 8.4 all_gather.75
  701.9 48.0 %while.51 = (s32[]{:T(128)}, f32[2,128,16,64]{1,3,2,0:T(8,128)S(1)}, f32[2,128,16,64]{1,3,2,0:T(8,128)}, bf16[2,2,512,16,64]{2,4,3,1,0:T(8,128)(2,1)}, s32[2,512...) while((s32[]{:T(128)}, ...), condition=%wide.region_12.13_spmd.clone, body=%wide.region_11.12_spmd.clone.sunk | while | flops 1100287488 | bytes 39723684 | solution.py:305
  708.5 11.0 fusion.246
  732.4 10.7 fusion.246
  758.9 10.5 pad_maximum_fusion
  770.0 11.4 all-gather.6
  782.0 9.6 all-gather.5
  792.9 16.3 %reduce-scatter.5.cloned.1.call-done = bf16[256,5120]{0,1:T(8,128)(2,1)} async-done(((bf16[1024,5120]{0,1:T(8,128)(2,1)}), bf16[256,5120]{0,1:T(8,128)(2,1)}) %reduce-scatter.5.cloned.1.call-update) | async-done | bytes 2621456 | tf_op jit(solution)/shard_map/reduce_scatter | solution.py:339
  809.1 248.9 %reduce-scatter.3.cloned.1.call-done = bf16[256,7168]{1,0:T(8,128)(2,1)} async-done(((bf16[1024,7168]{1,0:T(8,128)(2,1)}), bf16[256,7168]{1,0:T(8,128)(2,1)}) %reduce-scatter.3.cloned.1.call-update) | async-done | bytes 3670032 | tf_op jit(solution)/shard_map/reduce_scatter | solution.py:345
  1080.3 42.5 %all-reduce.2 = (f32[1024]{0:T(1024)S(1)}, f32[1024]{0:T(1024)S(1)}, f32[1024]{0:T(1024)S(1)}, f32[1024]{0:T(1024)S(1)}, f32[2048]{0:T(1024)S(1)}, /*index=5*/f3...) all-reduce(f32[1024]{0:T(1024)S(1)} %get-tuple-element.477, ...), channel_id=1, replica_groups=mesh['ctx'=8,'fsdp'=4] {'ctx','fsdp'}, use_global_device_ids=true, to_apply=%region_18.19 | all-reduce | flops 11520 | bytes 92160 | tf_op jit(solution)/shard_map/psum | solution.py:359
  1130.1 37.1 %all-reduce.6.cloned.1.call-done = (bf16[256,7168]{1,0:T(8,128)(2,1)}, bf16[256,5120]{0,1:T(8,128)(2,1)}) async-done(((bf16[256,7168]{1,0:T(8,128)(2,1)}, bf16[256,5120]{0,1:T(8,128)(2,1)}), (bf16[256,7168]{1,0:T(8,128)(2,1)}, bf16[256,5120]{0,1:T(8,128)(2,1)})) %all-reduce.6.cloned.1.call-update) | async-done | bytes 6291472 | tf_op jit(solution)/shard_map/psum | solution.py:353
  (310 shorter events, 253.1 us)
Async XLA Ops:
  7.2 46.5 %copy-start.48 = (u32[32]{0:T(128)S(1)}, u32[32]{0:T(128)}, u32[]{:S(2)}) copy-start(u32[32]{0:T(128)} %constant.185) | copy-start | bytes 388
  7.2 15.6 %copy-start.42 = (bf16[256]{0:T(256)(128)(2,1)S(1)}, bf16[256]{0:T(256)(128)(2,1)}, u32[]{:S(2)}) copy-start(bf16[256]{0:T(256)(128)(2,1)} %param.25) | copy-start | bytes 1540
  7.2 23.7 %copy-start.43 = (bf16[256]{0:T(256)(128)(2,1)S(1)}, bf16[256]{0:T(256)(128)(2,1)}, u32[]{:S(2)}) copy-start(bf16[256]{0:T(256)(128)(2,1)} %param.28) | copy-start | bytes 1540
  7.2 37.7 %copy-start.44 = (bf16[256]{0:T(256)(128)(2,1)S(1)}, bf16[256]{0:T(256)(128)(2,1)}, u32[]{:S(2)}) copy-start(bf16[256]{0:T(256)(128)(2,1)} %param.27) | copy-start | bytes 1540
  7.2 46.4 %copy-start.40 = (bf16[512]{0:T(512)(128)(2,1)S(1)}, bf16[512]{0:T(512)(128)(2,1)}, u32[]{:S(2)}) copy-start(bf16[512]{0:T(512)(128)(2,1)} %param.30) | copy-start | bytes 3076
  7.2 47.7 %copy-start.45 = (bf16[64]{0:T(256)(128)(2,1)S(1)}, bf16[64]{0:T(256)(128)(2,1)}, u32[]{:S(2)}) copy-start(bf16[64]{0:T(256)(128)(2,1)} %param.31) | copy-start | bytes 388
  7.3 80.9 %copy-start.3 = (bf16[2,128,1024]{2,1,0:T(8,128)(2,1)S(1)}, bf16[2,128,1024]{2,1,0:T(8,128)(2,1)}, u32[]{:S(2)}) copy-start(bf16[2,128,1024]{2,1,0:T(8,128)(2,1)} %param.23) | copy-start | bytes 1572868
  7.3 121.0 %all-gather.16.cloned.1.call-start = ((), (), s32[]{:S(2)}) async-start(), calls=%async_computation.2 | async-start | bytes 7864320 | tf_op jit(solution)/shard_map/all_gather | solution.py:150
  8.0 165.8 %all-gather.24.cloned.1.call-start = ((), (), s32[]{:S(2)}) async-start(), calls=%async_computation.6 | async-start | bytes 2621440 | tf_op jit(solution)/shard_map/all_gather | solution.py:152
  8.7 315.1 %all-gather.26.cloned.1.call-start = ((), (), s32[]{:S(2)}) async-start(), calls=%async_computation.7 | async-start | bytes 10485760 | tf_op jit(solution)/shard_map/all_gather | solution.py:153
  9.5 463.6 %all-gather.22.cloned.1.call-start = ((), (), s32[]{:S(2)}) async-start(), calls=%async_computation.5 | async-start | bytes 10485760 | tf_op jit(solution)/shard_map/all_gather | solution.py:151
  10.1 500.9 %all-gather.18.cloned.1.call-start = ((), (), s32[]{:S(2)}) async-start(), calls=%async_computation.3 | async-start | bytes 4718592 | tf_op jit(solution)/shard_map/all_gather | solution.py:174
  30.9 102.0 %copy-start.22 = (f32[4,1,256]{2,1,0:T(1,128)}, f32[4,1,256]{2,1,0:T(1,128)S(1)}, u32[]{:S(2)}) copy-start(f32[4,1,256]{2,1,0:T(1,128)S(1)} %convert_element_type.155) | copy-start | bytes 12292
  53.6 79.2 %copy-start.24 = (f32[4,1,256]{2,1,0:T(1,128)}, f32[4,1,256]{2,1,0:T(1,128)S(1)}, u32[]{:S(2)}) copy-start(f32[4,1,256]{2,1,0:T(1,128)S(1)} %convert_element_type.158) | copy-start | bytes 12292
  90.4 42.5 %copy-start.9 = (bf16[256,1024]{1,0:T(8,128)(2,1)}, bf16[256,1024]{1,0:T(8,128)(2,1)S(1)}, u32[]{:S(2)}) copy-start(bf16[256,1024]{1,0:T(8,128)(2,1)S(1)} %get-tuple-element.594) | copy-start | bytes 1572868
  135.6 414.5 %all-gather.20.cloned.1.call-start = ((), (), s32[]{:S(2)}) async-start(), calls=%async_computation.4 | async-start | bytes 4718592 | tf_op jit(solution)/shard_map/all_gather | solution.py:173
  135.8 9.0 copy-start.28
  148.7 509.0 %all-gather.28.cloned.1.call-start = ((), (), s32[]{:S(2)}) async-start(), calls=%async_computation.8 | async-start | bytes 4718592 | tf_op jit(solution)/shard_map/all_gather | solution.py:264
  150.7 538.0 %all-gather.30.cloned.1.call-start = ((), (), s32[]{:S(2)}) async-start(), calls=%async_computation.9 | async-start | bytes 4718592 | tf_op jit(solution)/shard_map/all_gather | solution.py:265
  177.0 155.2 %copy-start.6 = (bf16[2,128,1024]{2,1,0:T(8,128)(2,1)S(1)}, bf16[2,128,1024]{2,1,0:T(8,128)(2,1)}, u32[]{:S(2)}) copy-start(bf16[2,128,1024]{2,1,0:T(8,128)(2,1)} %param.24) | copy-start | bytes 1572868
  342.4 466.7 %reduce-scatter.5.cloned.1.call-start = ((), (), s32[]{:S(2)}) async-start(), calls=%async_computation.11 | async-start | bytes 13107200 | tf_op jit(solution)/shard_map/reduce_scatter | solution.py:339
  612.0 446.1 %reduce-scatter.3.cloned.1.call-start = ((), (), s32[]{:S(2)}) async-start(), calls=%async_computation.10 | async-start | bytes 18350080 | tf_op jit(solution)/shard_map/reduce_scatter | solution.py:345
  701.9 48.9 %copy-start.27 = (f32[128,8]{0,1:T(8,128)S(1)}, f32[128,8]{0,1:T(8,128)}, u32[]{:S(2)}) copy-start(f32[128,8]{0,1:T(8,128)} %copy-done.26) | copy-start | bytes 12292
  701.9 48.9 %copy-start.29 = (f32[128,8]{0,1:T(8,128)S(1)}, f32[128,8]{0,1:T(8,128)}, u32[]{:S(2)}) copy-start(f32[128,8]{0,1:T(8,128)} %copy-done.28) | copy-start | bytes 12292
  769.4 12.6 %copy-start.47 = (bf16[256]{0:T(256)(128)(2,1)S(1)}, bf16[256]{0:T(256)(128)(2,1)}, u32[]{:S(2)}) copy-start(bf16[256]{0:T(256)(128)(2,1)} %param.33) | copy-start | bytes 1540
  769.4 22.8 %copy-start.7 = (bf16[2,128,1024]{2,1,0:T(8,128)(2,1)S(1)}, bf16[2,128,1024]{2,1,0:T(8,128)(2,1)}, u32[]{:S(2)}) copy-start(bf16[2,128,1024]{2,1,0:T(8,128)(2,1)} %param.24) | copy-start | bytes 1572868
  769.4 397.8 %all-reduce.6.cloned.1.call-start = ((), (), s32[]{:S(2)}) async-start(), calls=%async_computation.12 | async-start | bytes 12582912 | tf_op jit(solution)/shard_map/psum | solution.py:353
  1073.1 54.1 %copy-start.8 = (bf16[2,128,1024]{2,1,0:T(8,128)(2,1)S(1)}, bf16[2,128,1024]{2,1,0:T(8,128)(2,1)}, u32[]{:S(2)}) copy-start(bf16[2,128,1024]{2,1,0:T(8,128)(2,1)} %param.24) | copy-start | bytes 1572868
  1073.1 54.1 %copy-start.17 = (f32[256,1024]{1,0:T(8,128)S(1)}, f32[256,1024]{1,0:T(8,128)}, u32[]{:S(2)}) copy-start(f32[256,1024]{1,0:T(8,128)} %fusion.159) | copy-start | bytes 3145732
  1073.2 54.1 %copy-start.33 = (f32[256]{0:T(256)S(1)}, f32[256]{0:T(256)}, u32[]{:S(2)}) copy-start(f32[256]{0:T(256)} %copy-done.32) | copy-start | bytes 3076
  1073.2 54.1 %copy-start.35 = (f32[256]{0:T(256)S(1)}, f32[256]{0:T(256)}, u32[]{:S(2)}) copy-start(f32[256]{0:T(256)} %copy-done.34) | copy-start | bytes 3076
  1125.4 57.1 %copy-start.38 = (f32[256]{0:T(256)}, f32[256]{0:T(256)S(1)}, u32[]{:S(2)}) copy-start(f32[256]{0:T(256)S(1)} %dynamic_slice.78) | copy-start | bytes 3076
  (34 other events, 170.5 us)
Sparse Core Ops, SparseCore 0:
  9.6 118.5 all-gather.15
  129.8 43.9 all-gather.23
  175.4 148.4 all-gather.25
  325.3 147.7 all-gather.21
  475.4 35.5 all-gather.17
  512.7 37.3 all-gather.19
  551.9 37.3 all-gather.27
  591.2 37.3 all-gather.29
  630.9 178.1 reduce-scatter.4
  811.3 246.6 reduce-scatter.2
  1061.5 105.6 all-reduce.5
where the time goes:
time: 1200 us; the launch traced here: 1190 us
  waiting for transfers between devices  685 us (57%)
  blocking collectives  170 us (14%)
  matrix products  158 us (13%)
  local copies, waits for them, and re-layouts  119 us (10%)
  other arithmetic  39.7 us (3%)
  between operations  15.8 us (1%)
    reduce_scatter x1, waiting for transfers between devices, per_device(): lax.psum_scatter(in_term(jnp.int32(0), row_count * lax.axis_size('fsdp'))...  249 us
    all_gather x1, waiting for transfers between devices, per_device(): lax.all_gather(ff_out_weight, 'fsdp', axis=0, tiled=True)  147 us
    all_gather x1, waiting for transfers between devices, per_device(): lax.all_gather(ff_in_weight, 'fsdp', axis=0, tiled=True)  130 us
    unnamed x136, local copies, waits for them, and re-layouts  45.5 us
    psum x1, blocking collectives, per_device(): lax.psum((gain_grad_one, shift_grad_one, gain_grad_two, shift_grad_two, q...  42.5 us
    all_gather x1, waiting for transfers between devices, per_device(): lax.all_gather(qkv_weight, 'fsdp', axis=0, tiled=True)  37.9 us
    psum x1, waiting for transfers between devices, per_device(): lax.psum(in_part.astype(jnp.bfloat16), 'ctx').astype(jnp.float32)  37.1 us
    reshape x4, local copies, waits for them, and re-layouts, blocked(): matrix.reshape(seq_count, blocks, key_block, H, HD).transpose(1, 0, 2, 3, 4)  31.5 us
  transfers between devices with their start and end apart: 11, of which 9 were waited for; matrix products, arithmetic and copies ran while one was open for 25% of the time, Pallas kernels for 0%

commit v1 on v0

v1 whole, which is shorter than its diff:
```python
import math

import jax
import jax.numpy as jnp
from jax import lax
from jax.experimental import pallas as pl
from jax.experimental.pallas import tpu as pltpu
from jax.sharding import PartitionSpec as P

D = 1024
H = 16
HD = 64
ROT = 16


EPSILON = 1e-05


def gelu_parts(inputs):
    cumulative = 0.5 * (1.0 + lax.erf(inputs * (1.0 / math.sqrt(2.0))))
    density = jnp.exp(-0.5 * inputs * inputs) * (1.0 / math.sqrt(2.0 * math.pi))
    return (inputs * cumulative, cumulative + inputs * density)


def rows_dot(left, right):
    return lax.dot_general(
        left, right, (((0,), (0,)), ((), ())), preferred_element_type=jnp.float32
    )


def cols_dot(left, right):
    return lax.dot_general(
        left, right, (((1,), (1,)), ((), ())), preferred_element_type=jnp.float32
    )


def rotary_wide(positions, width):
    halfway = ROT // 2
    lane = jnp.arange(width, dtype=jnp.int32) % HD
    step = (lane % halfway).astype(jnp.float32)
    frequency = jnp.exp(step * (-2.0 * math.log(10000.0) / ROT))
    theta = positions.astype(jnp.float32)[:, None] * frequency[None, :]
    cosine = jnp.where(lane < ROT, jnp.cos(theta), 1.0)
    sine = jnp.sin(theta)
    low = jnp.where(lane < halfway, sine, 0.0)
    high = jnp.where((lane >= halfway) & (lane < ROT), sine, 0.0)
    return cosine, low, high


def shifted(inputs, amount):
    return jnp.roll(inputs, -amount, axis=-1)


def attention_kernel(q_ref, k_ref, v_ref, do_ref, o_ref, dq_ref, dk_ref, dv_ref, ds_s, pw_s):
    groups = q_ref.shape[0]
    tokens = q_ref.shape[2]
    half = tokens // 2
    width = q_ref.shape[3]
    length = groups * tokens
    tile = min(256, length)

    def natural(ref, lanes):
        pieces = [ref[c, 0, 0:half, lanes] for c in range(groups)]
        pieces += [ref[c, 0, half:tokens, lanes] for c in reversed(range(groups))]
        return jnp.concatenate(pieces, axis=0)

    def put(ref, lanes, first, values):
        for i in range(values.shape[0] // half):
            b = first // half + i
            piece = values[i * half : (i + 1) * half].astype(ref.dtype)
            if b < groups:
                ref[b, 0, 0:half, lanes] = piece
            else:
                ref[2 * groups - 1 - b, 0, half:tokens, lanes] = piece

    for head in range(width // HD):
        lanes = slice(head * HD, (head + 1) * HD)
        q = natural(q_ref, lanes)
        k = natural(k_ref, lanes)
        v = natural(v_ref, lanes)
        do = natural(do_ref, lanes)
        row = lax.broadcasted_iota(jnp.int32, (tile, tile), 0)
        col = lax.broadcasted_iota(jnp.int32, (tile, tile), 1)
        allowed = col <= row
        for i in range(length // tile):
            start = i * tile
            stop = start + tile
            q_i = q[start:stop]
            do_i = do[start:stop]
            scores = cols_dot(q_i, k[:stop]) * 0.125
            diag = jnp.where(allowed, scores[:, start:stop], -1e30)
            scores = jnp.concatenate([scores[:, :start], diag], axis=1) if start else diag
            highest = jnp.max(scores, axis=-1, keepdims=True)
            powers = jnp.exp(scores - highest)
            total = jnp.sum(powers, axis=-1, keepdims=True)
            probs = powers * (1.0 / total)
            weights = probs.astype(jnp.bfloat16)
            mixed = jnp.dot(weights, v[:stop], preferred_element_type=jnp.float32)
            mixed_b = mixed.astype(jnp.bfloat16)
            delta = jnp.sum(
                do_i.astype(jnp.float32) * mixed_b.astype(jnp.float32), axis=-1, keepdims=True
            )
            dprobs = cols_dot(do_i, v[:stop])
            dscores = (probs * (dprobs - delta)).astype(jnp.bfloat16)
            dq = jnp.dot(dscores, k[:stop], preferred_element_type=jnp.float32) * 0.125
            put(o_ref, lanes, start, mixed_b)
            put(dq_ref, lanes, start, dq)
            pw_s[start:stop, :stop] = weights
            ds_s[start:stop, :stop] = dscores
        for j in range(length // tile):
            start = j * tile
            stop = start + tile
            dk = rows_dot(ds_s[start:, start:stop], q[start:]) * 0.125
            dv = rows_dot(pw_s[start:, start:stop], do[start:])
            put(dk_ref, lanes, start, dk)
            put(dv_ref, lanes, start, dv)


def attention(q, k, v, do):
    groups, seqs, tokens, width = q.shape
    length = groups * tokens
    spec = pl.BlockSpec((groups, 1, tokens, width), lambda i: (0, i, 0, 0))
    shape = (groups, seqs, tokens, width)
    return pl.pallas_call(
        attention_kernel,
        grid=(seqs,),
        in_specs=[spec] * 4,
        out_specs=[spec] * 4,
        out_shape=[jax.ShapeDtypeStruct(shape, jnp.bfloat16)]
        + [jax.ShapeDtypeStruct(shape, jnp.float32)] * 3,
        scratch_shapes=[pltpu.VMEM((length, length), jnp.bfloat16)] * 2,
        compiler_params=pltpu.CompilerParams(vmem_limit_bytes=50 * 1024 * 1024),
        name="attention",
    )(q, k, v, do)


def per_device(
    layer_in,
    cotangent,
    norm1_gain,
    norm1_shift,
    norm2_gain,
    norm2_shift,
    qkv_weight,
    qv_bias,
    key_bias,
    attn_out_weight,
    attn_out_bias,
    ff_in_weight,
    ff_in_bias,
    ff_out_weight,
    ff_out_bias,
):
    groups = lax.axis_size("ctx")
    shards = lax.axis_size("fsdp")
    place = lax.axis_index("ctx")
    seqs, tokens = layer_in.shape[:2]
    half = tokens // 2
    rows = groups * seqs * tokens
    wide = D // groups
    hidden = ff_in_weight.shape[1] // groups
    share = D // shards
    cut = lambda m, base, n: lax.dynamic_slice_in_dim(m, base + place * n, n, m.ndim - 1)

    small = (
        norm1_gain, norm1_shift, norm2_gain, norm2_shift,
        qv_bias, key_bias, attn_out_bias, ff_in_bias, ff_out_bias,
    )
    packed = jnp.concatenate(small)
    extra = -(-packed.shape[0] // (4 * wide * 16)) * 16
    packed = jnp.pad(packed, (0, extra * 4 * wide - packed.shape[0])).reshape(extra, 4 * wide)
    attn_cols = jnp.concatenate(
        [cut(qkv_weight, 0, wide), cut(qkv_weight, D, wide), cut(qkv_weight, 2 * D, wide),
         cut(attn_out_weight, 0, wide)], axis=1)
    attn_cols = jnp.concatenate([attn_cols, packed], axis=0)
    ff_cols = jnp.concatenate([cut(ff_in_weight, 0, hidden), cut(ff_out_weight, 0, hidden)], axis=1)
    x_all = lax.all_gather(layer_in, "ctx", axis=0)
    attn_full = lax.all_gather(attn_cols, "fsdp", axis=0)
    dy_all = lax.all_gather(cotangent, "ctx", axis=0)
    ff_full = lax.all_gather(ff_cols, "fsdp", axis=0, tiled=True)
    flat = attn_full[:, share:].reshape(shards, extra * 4 * wide).astype(jnp.float32)
    vectors = []
    start = 0
    for piece in small:
        n = piece.shape[0]
        vectors.append(flat[:, start : start + n].reshape(shards * n))
        start += n
    gain_one, shift_one, gain_two, shift_two, qv_all, key_all, attn_bias, ff_bias, out_bias = vectors
    attn_full = attn_full[:, :share].reshape(D, 4 * wide)
    qkv_w, ao_w = attn_full[:, : 3 * wide], attn_full[:, 3 * wide :]
    fi_w, fo_w = ff_full[:, :hidden], ff_full[:, hidden:]
    key_bias_full = jnp.pad(key_all.reshape(H, ROT), ((0, 0), (0, HD - ROT))).reshape(D)
    in_bias = jnp.concatenate(
        [cut(qv_all, 0, wide), cut(key_bias_full, 0, wide), cut(qv_all, D, wide)])
    ff_bias_own = cut(ff_bias, 0, hidden)

    x = x_all.reshape(rows, D).astype(jnp.float32)
    dy = dy_all.reshape(rows, D)
    average = jnp.mean(x, axis=-1, keepdims=True)
    centred = x - average
    inverse = lax.rsqrt(jnp.mean(centred * centred, axis=-1, keepdims=True) + EPSILON)
    unit = centred * inverse
    one_b = (unit * gain_one + shift_one).astype(jnp.bfloat16)
    two_b = (unit * gain_two + shift_two).astype(jnp.bfloat16)

    device_of = jnp.arange(groups, dtype=jnp.int32)[:, None]
    within = jnp.arange(tokens, dtype=jnp.int32)[None, :]
    pos = jnp.where(
        within < half,
        device_of * half + within,
        2 * half * groups - (device_of + 2) * half + within,
    ).reshape(groups * tokens)
    cosine, low, high = [
        t.reshape(groups, 1, tokens, 2 * wide) for t in rotary_wide(pos, 2 * wide)]
    projected = jnp.dot(one_b, qkv_w, preferred_element_type=jnp.float32) + in_bias
    projected = projected.reshape(groups, seqs, tokens, 3 * wide)
    qk = projected[..., : 2 * wide]
    halfway = ROT // 2
    qk = (qk * cosine - shifted(qk, halfway) * low + shifted(qk, -halfway) * high).astype(
        jnp.bfloat16)
    values = projected[..., 2 * wide :].astype(jnp.bfloat16)
    dout = jnp.dot(dy, ao_w, preferred_element_type=jnp.float32).astype(jnp.bfloat16)
    dout = dout.reshape(groups, seqs, tokens, wide)
    mixed, dq, dk, dv = attention(qk[..., :wide], qk[..., wide:], values, dout)
    dqk = jnp.concatenate([dq, dk], axis=-1)
    dqk = dqk * cosine + shifted(dqk, halfway) * low - shifted(dqk, -halfway) * high
    dproj = jnp.concatenate([dqk, dv], axis=-1).reshape(rows, 3 * wide)
    dproj_b = dproj.astype(jnp.bfloat16)

    hpre = jnp.dot(two_b, fi_w, preferred_element_type=jnp.float32) + ff_bias_own
    activation, slope = gelu_parts(hpre)
    gelu_b = activation.astype(jnp.bfloat16)
    dpre = jnp.dot(dy, fo_w, preferred_element_type=jnp.float32) * slope
    dpre_b = dpre.astype(jnp.bfloat16)
    ff_terms = jnp.concatenate([rows_dot(two_b, dpre_b), rows_dot(dy, gelu_b)], axis=1)
    ff_own = lax.psum_scatter(
        ff_terms.astype(jnp.bfloat16), "fsdp", scatter_dimension=0, tiled=True)

    mixed = mixed.reshape(rows, wide)
    out_part = cols_dot(mixed, ao_w) + cols_dot(gelu_b, fo_w)
    out_sum = lax.psum_scatter(
        out_part.astype(jnp.bfloat16).reshape(groups, seqs, tokens, D), "ctx", scatter_dimension=0)
    layer_out = (
        layer_in.astype(jnp.float32) + out_sum.astype(jnp.float32) + attn_bias + out_bias
    ).astype(jnp.bfloat16)

    dn_one = cols_dot(dproj_b, qkv_w)
    dn_two = cols_dot(dpre_b, fi_w)
    scaled_part = (dn_one * gain_one + dn_two * gain_two).astype(jnp.bfloat16)
    scaled = lax.psum_scatter(
        scaled_part.reshape(groups, seqs, tokens, D), "ctx", scatter_dimension=0
    ).astype(jnp.float32)
    x_own = layer_in.astype(jnp.float32)
    mean_own = jnp.mean(x_own, axis=-1, keepdims=True)
    centred_own = x_own - mean_own
    inverse_own = lax.rsqrt(jnp.mean(centred_own * centred_own, axis=-1, keepdims=True) + EPSILON)
    unit_own = centred_own * inverse_own
    input_grad = cotangent.astype(jnp.float32) + inverse_own * (
        scaled
        - jnp.mean(scaled, axis=-1, keepdims=True)
        - unit_own * jnp.mean(scaled * unit_own, axis=-1, keepdims=True)
    )

    def spread(vector, total, base):
        whole = lax.dynamic_update_slice_in_dim(
            jnp.zeros((total,), jnp.float32), vector, base + place * vector.shape[0], 0)
        return whole.reshape(shards, total // shards)

    colsum = jnp.sum(dproj, axis=0)
    key_cols = colsum[wide : 2 * wide].reshape(wide // HD, HD)[:, :ROT].reshape(-1)
    pieces = [
        jnp.sum(dn_one * unit, axis=0).reshape(shards, share),
        jnp.sum(dn_one, axis=0).reshape(shards, share),
        jnp.sum(dn_two * unit, axis=0).reshape(shards, share),
        jnp.sum(dn_two, axis=0).reshape(shards, share),
        spread(colsum[:wide], 2 * D, 0) + spread(colsum[2 * wide :], 2 * D, D),
        spread(key_cols, H * ROT, 0),
        jnp.sum(cotangent.astype(jnp.float32), axis=(0, 1)).reshape(shards, share),
        spread(jnp.sum(dpre, axis=0), hidden * groups, 0),
    ]
    packed_grads = jnp.concatenate(pieces, axis=1)
    used = packed_grads.shape[1]
    more = -(-used // (4 * wide * 16)) * 16
    packed_grads = jnp.pad(packed_grads, ((0, 0), (0, more * 4 * wide - used)))
    attn_terms = jnp.concatenate([rows_dot(one_b, dproj_b), rows_dot(dy, mixed)], axis=1)
    attn_terms = jnp.concatenate(
        [attn_terms.reshape(shards, share, 4 * wide), packed_grads.reshape(shards, more, 4 * wide)],
        axis=1)
    attn_own = lax.psum_scatter(attn_terms.astype(jnp.bfloat16), "fsdp", scatter_dimension=0)
    ff_grads = lax.all_gather(ff_own, "ctx", axis=0)
    attn_grads = lax.all_gather(attn_own, "ctx", axis=0)

    def side_by_side(stacked):
        return stacked.transpose(1, 0, 2).reshape(share, -1).astype(jnp.float32)

    matrices = attn_grads[:, :share]
    qkv_grad = jnp.concatenate(
        [side_by_side(matrices[..., i * wide : (i + 1) * wide]) for i in range(3)], axis=1)
    ao_grad = side_by_side(matrices[..., 3 * wide :])
    fi_grad = side_by_side(ff_grads[..., :hidden])
    fo_grad = side_by_side(ff_grads[..., hidden:])
    vec = jnp.sum(attn_grads[:, share:].astype(jnp.float32), axis=0).reshape(-1)
    shares = []
    start = 0
    for piece in pieces:
        shares.append(vec[start : start + piece.shape[1]])
        start += piece.shape[1]
    return (
        layer_out,
        input_grad,
        shares[0],
        shares[1],
        shares[2],
        shares[3],
        qkv_grad,
        shares[4],
        shares[5],
        ao_grad,
        shares[6],
        fi_grad,
        shares[7],
        fo_grad,
        shares[6],
    )


def solution(mesh):
    placed = (
        P("fsdp", "ctx", None),
        P("fsdp", "ctx", None),
        P("fsdp"),
        P("fsdp"),
        P("fsdp"),
        P("fsdp"),
        P("fsdp", None),
        P("fsdp"),
        P("fsdp"),
        P("fsdp", None),
        P("fsdp"),
        P("fsdp", None),
        P("fsdp"),
        P("fsdp", None),
        P("fsdp"),
    )
    return jax.shard_map(
        per_device,
        mesh=mesh,
        in_specs=placed,
        out_specs=(
            P("fsdp", "ctx", None),
            P("fsdp", "ctx", None),
            P("fsdp"),
            P("fsdp"),
            P("fsdp"),
            P("fsdp"),
            P("fsdp", None),
            P("fsdp"),
            P("fsdp"),
            P("fsdp", None),
            P("fsdp"),
            P("fsdp", None),
            P("fsdp"),
            P("fsdp", None),
            P("fsdp"),
        ),
        check_vma=False,
    )
```

time: 1200 us -> 496 us (0.41)
  waiting for transfers between devices: 685 us -> 292 us
  blocking collectives: 170 us -> 0 us
  matrix products: 158 us -> 49.2 us
  local copies, waits for them, and re-layouts: 119 us -> 69.8 us
  Pallas kernels: 0 us -> 19.4 us
    all_gather x8 -> x6, waiting for transfers between devices: 380 us -> 143 us  [the longest x1 36.3 us: per_device(): ff_grads = lax.all_gather(ff_own, 'ctx', axis=0)]
    reduce_scatter x2 -> x4, waiting for transfers between devices: 265 us -> 146 us  [the longest x1 52.5 us: per_device(): lax.psum_scatter(out_part.astype(jnp.bfloat16).reshape(groups, seqs, toke...]
    all_gather x10 -> x0, blocking collectives: 117 us -> none  [the longest x1 22.4 us: per_device(): lax.all_gather(qv_bias, 'fsdp', axis=0, tiled=True)]
    dot_general x23 -> x12, matrix products: 158 us -> 49.2 us  [the longest x4 16.2 us: cols_dot(): lax.dot_general(left, right, (((1,), (1,)), ((), ())), preferred_element_...]
    psum x1 -> x0, blocking collectives: 42.5 us -> none  [per_device(): lax.psum((gain_grad_one, shift_grad_one, gain_grad_two, shift_grad_two, q...]
    psum x1 -> x0, waiting for transfers between devices: 37.1 us -> none  [per_device(): lax.psum(in_part.astype(jnp.bfloat16), 'ctx').astype(jnp.float32)]
    reshape x13 -> x12, local copies, waits for them, and re-layouts: 35.1 us -> 1.75 us  [the longest x1 1.32 us: per_device(): attn_terms.reshape(shards, share, 4 * wide)]
    pallas_call x0 -> x1, Pallas kernels: none -> 19.4 us  [attention(): pl.pallas_call(attention_kernel, grid=(seqs,), in_specs=[spec] * 4, out_s...]
  transfers between devices with their start and end apart: 11 -> 10, of which waited for: 9 -> 10; matrix products, arithmetic and copies ran while one was open for 25% -> 19% of each run, Pallas kernels for 0% -> 4%
where the time goes in v1:
time: 496 us; the launch traced here: 488 us
  waiting for transfers between devices  292 us (59%)
  local copies, waits for them, and re-layouts  69.8 us (14%)
  matrix products  49.2 us (10%)
  other arithmetic  41.4 us (8%)
  Pallas kernels  19.4 us (4%)
  between operations  15 us (3%)
    reduce_scatter x1, waiting for transfers between devices, per_device(): lax.psum_scatter(out_part.astype(jnp.bfloat16).reshape(groups, seqs, toke...  52.5 us
    reduce_scatter x1, waiting for transfers between devices, per_device(): lax.psum_scatter(scaled_part.reshape(groups, seqs, tokens, D), 'ctx', sca...  40 us
    all_gather x1, waiting for transfers between devices, per_device(): ff_grads = lax.all_gather(ff_own, 'ctx', axis=0)  36.3 us
    reduce_scatter x1, waiting for transfers between devices, per_device(): lax.psum_scatter(ff_terms.astype(jnp.bfloat16), 'fsdp', scatter_dimension...  35.8 us
    all_gather x1, waiting for transfers between devices, per_device(): x_all = lax.all_gather(layer_in, 'ctx', axis=0)  34.1 us
    unnamed x83, local copies, waits for them, and re-layouts  31.4 us
    all_gather x1, waiting for transfers between devices, per_device(): attn_grads = lax.all_gather(attn_own, 'ctx', axis=0)  28.9 us
    all_gather x1, waiting for transfers between devices, per_device(): attn_full = lax.all_gather(attn_cols, 'fsdp', axis=0)  23 us
  transfers between devices with their start and end apart: 10, of which 10 were waited for; matrix products, arithmetic and copies ran while one was open for 19% of the time, Pallas kernels for 4%

profile of v1, /device:TPU:0, one launch (start us, length us, event | category | flops | bytes accessed | tf_op | source)
XLA Modules:
  0.0 487.6 jit_solution(4504223031842648629)
XLA Ops:
  7.2 6.2 %concatenate.58 = bf16[3136]{0:T(1024)(128)(2,1)S(1)} concatenate(bf16[256]{0:T(256)(128)(2,1)} %param.17, bf16[256]{0:T(256)(128)(2,1)} %param.18, bf16[256]{0:T(256)(128)(2,1)} %param.19, bf16[256]{0:T(256)(128)(2,1)} %param.20, bf16[512]{0:T(512)(128)(2,1)} %param.22, bf16[64]{0:T(256)(128)(2,1)} %param.23, bf16[256]{0:T(256)(128)(2,1)} %param.25, bf16[1024]{0:T(1024)(128)(2,1)} %param.27, ...), dimensions={0} | concatenate | bytes 12544 | tf_op jit(solution)/shard_map/concatenate | solution.py:169
  19.1 5.1 %fusion.34 = (f32[8,128,256]{2,1,0:T(8,128)}, f32[8,128,256]{2,1,0:T(8,128)}, f32[8,128,256]{2,1,0:T(8,128)}) fusion(f32[256]{0:T(256)S(1)} %fusion.56, f32[8,128]{1,0:T(8,128)S(1)} %fusion.53, pred[256]{0:T(512)(128)(4,1)S(1)} %broadcast_compare_fusion.1, pred[256]{0:T(512)(128)(4,1)S(1)} %get-tuple-element.91, pred[256]{0:T(512)(128)(4,1)S(1)} %get-tuple-element.90), kind=kLoop, calls=%fused_computation.71 | loop fusion | flops 1048576 | bytes 3151616 | tf_op jit(solution)/shard_map/jit(_where)/select_n | solution.py:43
  24.2 23.0 %all-gather.17.cloned.1.call-done = bf16[1088,512]{1,0:T(8,128)(2,1)} async-done(((bf16[272,512]{1,0:T(8,128)(2,1)}), bf16[1088,512]{1,0:T(8,128)(2,1)}) %all-gather.17.cloned.1.call-update) | async-done | bytes 1114128 | tf_op jit(solution)/shard_map/all_gather | solution.py:178
  50.9 34.1 %all-gather.15.cloned.1.call-done = bf16[16,128,1024]{2,1,0:T(8,128)(2,1)} async-done(((bf16[2,128,1024]{2,1,0:T(8,128)(2,1)}), bf16[16,128,1024]{2,1,0:T(8,128)(2,1)}) %all-gather.15.cloned.1.call-update) | async-done | bytes 4194320 | tf_op jit(solution)/shard_map/all_gather | solution.py:177
  85.1 3.0 convert_reduce_fusion
  88.5 3.9 multiply_reduce_fusion.2
  92.4 3.7 add_convert_fusion.4
  103.2 20.4 %all-gather.19.cloned.1.call-done = bf16[16,128,1024]{2,1,0:T(8,128)(2,1)} async-done(((bf16[2,128,1024]{2,1,0:T(8,128)(2,1)}), bf16[16,128,1024]{2,1,0:T(8,128)(2,1)}) %all-gather.19.cloned.1.call-update) | async-done | bytes 4194320 | tf_op jit(solution)/shard_map/all_gather | solution.py:179
  123.6 4.7 fusion.13
  128.3 3.8 fusion.16
  134.1 19.4 %attention.1 = (bf16[8,2,128,128]{3,2,1,0:T(8,128)(2,1)S(1)}, f32[8,2,128,128]{3,2,1,0:T(8,128)S(1)}, f32[8,2,128,128]{3,2,1,0:T(8,128)}, f32[8,2,128,128]{3,2,1,0:T(8,128)}) custom-call(bf16[8,2,128,128]{3,2,1,0:T(8,128)(2,1)S(1)} %get-tuple-element.65.q_ref, bf16[8,2,128,128]{3,2,1,0:T(8,128)(2,1)S(1)} %get-tuple-element.64.k_ref, ...), custom_call_target="tpu_custom_call" | custom-call | tf_op jit(solution)/shard_map/attention/pallas_call | solution.py:124
  162.7 5.6 %bitcast_convert_fusion = bf16[1024,384]{0,1:T(8,128)(2,1)S(1)} fusion(bf16[8,2,128,384]{3,2,1,0:T(8,128)(2,1)S(1)} %fusion.12, f32[8,2,128,1024]{3,2,1,0:T(8,128)} %get-tuple-element.43, f32[1024]{0:T(1024)S(1)} %bitcast.191, f32[1024]{0:T(1024)S(1)} %bitcast.188, f32[8,2,128]{2,1,0:T(2,128)S(1)} %add_rsqrt_fusion, f32[8,2,128]{2,1,0:T(2,128)S(1)} %bitcast.181), kind=kOutput, calls=%fused_computation.44 | convolution fusion | flops 1621491712 | bytes 10772480 | tf_op jit(solution)/shard_map/dot_general | solution.py:26
  170.7 6.9 %multiply_convert_fusion = (bf16[2048,512]{1,0:T(8,128)(2,1)}, f32[2048,512]{1,0:T(8,128)S(1)}) fusion(f32[512]{0:T(512)S(1)} %dynamic_slice.39, bf16[2048,1024]{1,0:T(8,128)(2,1)} %get-tuple-element.48, bf16[1024,1024]{1,0:T(8,128)(2,1)} %all-gather.11.cloned.1.call-done), kind=kOutput, calls=%fused_computation.23 | convolution fusion | flops 2153775104 | bytes 11536384 | tf_op jit(solution)/shard_map/dot_general | solution.py:230
  177.6 4.9 fusion.68
  186.2 6.3 %fusion.59 = (bf16[1024]{0:T(1024)(128)(2,1)S(1)}, bf16[1024]{0:T(1024)(128)(2,1)S(1)}, bf16[2048,1024]{1,0:T(8,128)(2,1)}, bf16[1024]{0:T(1024)(128)(2,1)S(1)}, bf16[1024]{0:T(1024)(128)(2,1)S(1)}) fusion(f32[2048]{0:T(1024)S(1)} %bitcast.183, f32[2048]{0:T(1024)S(1)} %get-tuple-element.81, bf16[16,128,1024]{2,1,0:T(8,128)(2,1)S(1)} %copy-done.1, ...), kind=kOutput, calls=%fused_computation.142 | convolution fusion | flops 2174742528 | bytes 19955712 | tf_op jit(solution)/shard_map/dot_general | solution.py:32
  194.3 5.4 %convolution_convert_fusion.2 = bf16[1024,512]{0,1:T(8,128)(2,1)S(1)} fusion(bf16[2048,1024]{1,0:T(8,128)(2,1)} %get-tuple-element.48, bf16[2048,512]{1,0:T(8,128)(2,1)} %get-tuple-element.89), kind=kOutput, calls=%fused_computation.51 | convolution fusion | flops 2148007936 | bytes 7340032 | tf_op jit(solution)/shard_map/dot_general | solution.py:26
  203.8 18.0 %reduce-scatter.9.cloned.1.call-done = bf16[1,272,512]{2,1,0:T(8,128)(2,1)} async-done(((bf16[4,272,512]{2,1,0:T(8,128)(2,1)}), bf16[1,272,512]{2,1,0:T(8,128)(2,1)}) %reduce-scatter.9.cloned.1.call-update) | async-done | bytes 278544 | tf_op jit(solution)/shard_map/reduce_scatter | solution.py:289
  222.6 4.2 fusion.42
  226.8 3.3 add_convert_fusion.2
  230.3 35.8 %reduce-scatter.11.cloned.1.call-done = bf16[256,1024]{0,1:T(8,128)(2,1)} async-done(((bf16[1024,1024]{0,1:T(8,128)(2,1)}), bf16[256,1024]{0,1:T(8,128)(2,1)}) %reduce-scatter.11.cloned.1.call-update) | async-done | bytes 524304 | tf_op jit(solution)/shard_map/reduce_scatter | solution.py:236
  266.6 28.9 %all-gather.13.cloned.1.call-done = bf16[8,272,512]{2,1,0:T(8,128)(2,1)} async-done(((bf16[1,272,512]{2,1,0:T(8,128)(2,1)}), bf16[8,272,512]{2,1,0:T(8,128)(2,1)}) %all-gather.13.cloned.1.call-update) | async-done | bytes 2228240 | tf_op jit(solution)/shard_map/all_gather | solution.py:291
  306.0 3.9 copy.72
  310.6 40.0 %reduce-scatter.7.cloned.1.call-done = bf16[1,2,128,1024]{3,2,1,0:T(8,128)(2,1)} async-done(((bf16[8,2,128,1024]{3,2,1,0:T(8,128)(2,1)}), bf16[1,2,128,1024]{3,2,1,0:T(8,128)(2,1)}) %reduce-scatter.7.cloned.1.call-update) | async-done | bytes 524304 | tf_op jit(solution)/shard_map/reduce_scatter | solution.py:250
  353.2 52.5 %reduce-scatter.5.cloned.1.call-done = bf16[1,2,128,1024]{3,2,1,0:T(8,128)(2,1)} async-done(((bf16[8,2,128,1024]{3,2,1,0:T(8,128)(2,1)}), bf16[1,2,128,1024]{3,2,1,0:T(8,128)(2,1)}) %reduce-scatter.5.cloned.1.call-update) | async-done | bytes 524304 | tf_op jit(solution)/shard_map/reduce_scatter | solution.py:241
  405.8 2.8 fusion.31
  408.6 36.3 %all-gather.21.cloned.1.call-done = bf16[2048,1024]{0,1:T(8,128)(2,1)} async-done(((bf16[256,1024]{0,1:T(8,128)(2,1)}), bf16[2048,1024]{0,1:T(8,128)(2,1)}) %all-gather.21.cloned.1.call-update) | async-done | bytes 4194320 | tf_op jit(solution)/shard_map/all_gather | solution.py:290
  444.9 3.7 copy.98
  448.6 4.1 convert_bitcast_fusion
  452.6 5.6 %copy.71 = f32[256,8,512]{2,1,0:T(8,128)} copy(f32[256,8,512]{0,1,2:T(8,128)} %get-tuple-element.49) | data formatting | bytes 8388608 | tf_op jit(solution)/shard_map/convert_element_type | solution.py:294
  458.2 8.0 %copy.100 = f32[32,8,8,512]{3,1,2,0:T(8,128)} copy(f32[32,8,8,512]{3,2,1,0:T(8,128)} %bitcast.152) | data formatting | bytes 8388608
  466.2 5.8 %copy.70 = f32[256,8,512]{2,1,0:T(8,128)} copy(f32[256,8,512]{0,1,2:T(8,128)} %get-tuple-element.50) | data formatting | bytes 8388608 | tf_op jit(solution)/shard_map/convert_element_type | solution.py:294
  471.9 8.0 %copy.99 = f32[32,8,8,512]{3,1,2,0:T(8,128)} copy(f32[32,8,8,512]{3,2,1,0:T(8,128)} %bitcast.153) | data formatting | bytes 8388608
  (181 shorter events, 55.5 us)
Async XLA Ops:
  7.2 11.7 %copy-start.17 = (bf16[2,128,1024]{2,1,0:T(8,128)(2,1)S(1)}, bf16[2,128,1024]{2,1,0:T(8,128)(2,1)}, u32[]{:S(2)}) copy-start(bf16[2,128,1024]{2,1,0:T(8,128)(2,1)} %param.16) | copy-start | bytes 1572868
  7.2 39.9 %all-gather.17.cloned.1.call-start = ((), (), s32[]{:S(2)}) async-start(), calls=%async_computation.11 | async-start | bytes 1392640 | tf_op jit(solution)/shard_map/all_gather | solution.py:178
  15.2 69.8 %all-gather.15.cloned.1.call-start = ((), (), s32[]{:S(2)}) async-start(), calls=%async_computation.10 | async-start | bytes 4718592 | tf_op jit(solution)/shard_map/all_gather | solution.py:177
  16.0 107.6 %all-gather.19.cloned.1.call-start = ((), (), s32[]{:S(2)}) async-start(), calls=%async_computation.12 | async-start | bytes 4718592 | tf_op jit(solution)/shard_map/all_gather | solution.py:179
  16.7 154.0 %all-gather.11.cloned.1.call-start = ((), (), s32[]{:S(2)}) async-start(), calls=%async_computation.4 | async-start | bytes 2621440 | tf_op jit(solution)/shard_map/all_gather | solution.py:180
  18.8 203.0 %reduce-scatter.9.cloned.1.call-start = ((), (), s32[]{:S(2)}) async-start(), calls=%async_computation.7 | async-start | bytes 1392640 | tf_op jit(solution)/shard_map/reduce_scatter | solution.py:289
  85.0 3.4 copy-start
  92.4 3.7 copy-start.15
  98.5 29.8 %copy-start.5 = (f32[2048,384]{1,0:T(8,128)}, f32[2048,384]{1,0:T(8,128)S(1)}, u32[]{:S(2)}) copy-start(f32[2048,384]{1,0:T(8,128)S(1)} %convolution_add_fusion) | copy-start | bytes 9437188
  123.6 4.8 copy-start.7
  123.6 4.8 copy-start.9
  123.6 4.8 copy-start.11
  123.6 4.8 copy-start.20
  159.4 2.5 copy-start.2
  170.7 6.9 %copy-start.3 = (bf16[16,128,1024]{2,1,0:T(8,128)(2,1)S(1)}, bf16[16,128,1024]{2,1,0:T(8,128)(2,1)}, u32[]{:S(2)}) copy-start(bf16[16,128,1024]{2,1,0:T(8,128)(2,1)} %all-gather.19.cloned.1.call-done) | copy-start | bytes 12582916
  170.7 6.9 %copy-start.25 = (bf16[1024,1024]{1,0:T(8,128)(2,1)S(1)}, bf16[1024,1024]{1,0:T(8,128)(2,1)}, u32[]{:S(2)}) copy-start(bf16[1024,1024]{1,0:T(8,128)(2,1)} %all-gather.11.cloned.1.call-done) | copy-start | bytes 6291460
  177.6 5.1 %copy-start.14 = (bf16[8,2,128,384]{3,2,1,0:T(8,128)(2,1)S(1)}, bf16[8,2,128,384]{3,2,1,0:T(8,128)(2,1)}, u32[]{:S(2)}) copy-start(bf16[8,2,128,384]{3,2,1,0:T(8,128)(2,1)} %copy-done.13) | copy-start | bytes 4718596
  177.6 5.1 %copy-start.16 = (bf16[4,256,512]{2,1,0:T(8,128)(2,1)S(1)}, bf16[4,256,512]{2,1,0:T(8,128)(2,1)}, u32[]{:S(2)}) copy-start(bf16[4,256,512]{2,1,0:T(8,128)(2,1)} %slice.215) | copy-start | bytes 3145732
  182.7 2.4 copy-start.1
  182.7 2.9 copy-start.26
  182.7 3.5 copy-start.28
  186.2 6.5 %copy-start.19 = (bf16[1024,512]{1,0:T(8,128)(2,1)S(1)}, bf16[1024,512]{1,0:T(8,128)(2,1)}, u32[]{:S(2)}) copy-start(bf16[1024,512]{1,0:T(8,128)(2,1)} %copy.79) | copy-start | bytes 3145732
  193.9 72.2 %reduce-scatter.11.cloned.1.call-start = ((), (), s32[]{:S(2)}) async-start(), calls=%async_computation.9 | async-start | bytes 2621440 | tf_op jit(solution)/shard_map/reduce_scatter | solution.py:236
  194.3 5.4 %copy-start.4 = (bf16[16,128,1024]{2,1,0:T(8,128)(2,1)S(1)}, bf16[16,128,1024]{2,1,0:T(8,128)(2,1)}, u32[]{:S(2)}) copy-start(bf16[16,128,1024]{2,1,0:T(8,128)(2,1)} %all-gather.19.cloned.1.call-done) | copy-start | bytes 12582916
  194.3 5.4 %copy-start.27 = (bf16[2048,512]{1,0:T(8,128)(2,1)S(1)}, bf16[2048,512]{1,0:T(8,128)(2,1)}, u32[]{:S(2)}) copy-start(bf16[2048,512]{1,0:T(8,128)(2,1)} %get-tuple-element.86) | copy-start | bytes 6291460
  203.7 91.8 %all-gather.13.cloned.1.call-start = ((), (), s32[]{:S(2)}) async-start(), calls=%async_computation.8 | async-start | bytes 2506752 | tf_op jit(solution)/shard_map/all_gather | solution.py:291
  221.8 128.9 %reduce-scatter.7.cloned.1.call-start = ((), (), s32[]{:S(2)}) async-start(), calls=%async_computation.6 | async-start | bytes 4718592 | tf_op jit(solution)/shard_map/reduce_scatter | solution.py:250
  222.5 183.3 %reduce-scatter.5.cloned.1.call-start = ((), (), s32[]{:S(2)}) async-start(), calls=%async_computation.5 | async-start | bytes 4718592 | tf_op jit(solution)/shard_map/reduce_scatter | solution.py:241
  230.1 36.0 %copy-start.6 = (bf16[2,128,1024]{2,1,0:T(8,128)(2,1)S(1)}, bf16[2,128,1024]{2,1,0:T(8,128)(2,1)}, u32[]{:S(2)}) copy-start(bf16[2,128,1024]{2,1,0:T(8,128)(2,1)} %param.15) | copy-start | bytes 1572868
  230.1 214.8 %all-gather.21.cloned.1.call-start = ((), (), s32[]{:S(2)}) async-start(), calls=%async_computation.13 | async-start | bytes 4718592 | tf_op jit(solution)/shard_map/all_gather | solution.py:290
  301.0 178.9 %copy-start.24 = (f32[256]{0:T(256)}, f32[256]{0:T(256)S(1)}, u32[]{:S(2)}) copy-start(f32[256]{0:T(256)S(1)} %get-tuple-element.128) | copy-start | bytes 3076
  306.0 99.7 %copy-start.18 = (bf16[2,128,1024]{2,1,0:T(8,128)(2,1)S(1)}, bf16[2,128,1024]{2,1,0:T(8,128)(2,1)}, u32[]{:S(2)}) copy-start(bf16[2,128,1024]{2,1,0:T(8,128)(2,1)} %param.16) | copy-start | bytes 1572868
  (7 other events, 11.0 us)
Sparse Core Ops, SparseCore 0:
  15.3 31.7 all-gather.16
  49.0 35.9 all-gather.14
  86.9 36.5 all-gather.18
  125.0 45.6 all-gather.10
  194.0 27.7 reduce-scatter.8
  223.9 42.1 reduce-scatter.10
  268.0 27.5 all-gather.12
  299.5 51.1 reduce-scatter.6
  354.6 51.1 reduce-scatter.4
  407.5 37.3 all-gather.20
